TPU v7x, 256 devices: a whole 4x4x8 slice. The times are simulated.
256 devices in a mesh: gy: 4 (over x), gx: 4 (over z_hi), ga: 16 (over y, z_lo, core).
Axes of the slice: x: 4, y: 4, z: 8 (z_hi: 4, z_lo: 2; z = z_hi * 2 + z_lo), core: 2. Of those that a mesh axis runs over, the one named last changes fastest.
Arguments:
- volume: bfloat16 [16, 56, 56, 7, 768], P('ga', 'gy', 'gx'), may hold values from -6 to 6
- affinity: bfloat16 [16, 3, 56, 56, 7], P('ga', None, 'gy', 'gx'), may hold values from 0 to 1
- window_dest: int32 [16, 4, 4, 4], P('ga', 'gy', 'gx'), may hold values from 0 to 16, as said below
- qkv_weight: bfloat16 [768, 1152], replicated
- proj_weight: bfloat16 [384, 768], replicated, may hold values from -0.3125 to 0.3125
- head_weight: bfloat16 [768, 3], replicated, may hold values from -0.21875 to 0.21875
Outputs:
- grad_volume: bfloat16 [16, 56, 56, 7, 768], P('ga', 'gy', 'gx')
- grad_qkv: float32 [768, 1152], P('ga')
- grad_proj: float32 [384, 768], P(None, 'ga')
Inputs may be any that keep to these rules, and one draw needn't show every extreme that they name: `window_dest`: 16 marks an empty window; any other value names the device along ga, with the same gy and gx, that computes the window: the device itself or one of the min(2, 15) devices after it, cyclically (index plus 1, plus 2, modulo 16). Every device computes exactly 2 live windows, receives at most 1 from any one device, and in every group some device has 4 live windows (all of its windows), keeps 2 of them and sends 1 to each of the 2 devices after it along ga.
All inputs are finite; a program needn't handle non-finite values.
Results may differ from a plain program's by a relative error of at most 0.0065.
The roundings to bfloat16 on the way count: a program that leaves them out, or rounds other values in their place, can miss the bound.
Values may be sent and summed in bfloat16 or wider, within the bound.
No kernel may reach another device: no remote copies, remote signals or barrier semaphores. Data moves between devices by JAX's collectives and lax.ppermute only.
A program may use at most 128 MiB of HBM per device.

v0:
```python
import jax
import jax.numpy as jnp
from jax import lax
from jax.sharding import PartitionSpec as P

HEAD = 32
WIN = 7
HOPS = 2
LOSS_SCALE = 32.0
EPSILON = 1e-05


def passed_along(block, axis, distance):
    devices = range(lax.axis_size(axis))
    route = [((i - distance) % len(devices), i) for i in devices]
    return lax.ppermute(block, axis, route)


def for_sending(value):
    return jax.tree.map(lambda a: a.astype(jnp.bfloat16) if a.dtype == jnp.float32 else a, value)


def window_grads(tokens, target, region, qkv_weight, proj_weight, head_weight):
    inner_width = proj_weight.shape[0]
    head_count = inner_width // HEAD
    token_count = tokens.shape[0]
    score_scale = HEAD ** (-0.5)
    floated = tokens.astype(jnp.float32)
    mean_row = jnp.mean(floated, axis=-1, keepdims=True)
    centred = floated - mean_row
    variance = jnp.mean(centred * centred, axis=-1, keepdims=True)
    inv_std = lax.rsqrt(variance + EPSILON)
    unit_rows = centred * inv_std
    normed = unit_rows.astype(jnp.bfloat16)
    projected = jnp.dot(normed, qkv_weight, preferred_element_type=jnp.float32).astype(jnp.bfloat16)
    queries = projected[:, :inner_width].reshape(token_count, head_count, HEAD)
    key_rows = projected[:, inner_width : 2 * inner_width].reshape(token_count, head_count, HEAD)
    values = projected[:, 2 * inner_width :].reshape(token_count, head_count, HEAD)
    scores = (
        jnp.einsum("qhd,khd->hqk", queries, key_rows, preferred_element_type=jnp.float32)
        * score_scale
    )
    allowed = region[:, None] == region[None, :]
    scores = jnp.where(allowed[None], scores, jnp.float32(-1e30))
    row_max = jnp.max(scores, axis=-1, keepdims=True)
    exponent = jnp.exp(scores - row_max)
    attend = exponent / jnp.sum(exponent, axis=-1, keepdims=True)
    attend_low = attend.astype(jnp.bfloat16)
    mixed = (
        jnp.einsum("hqk,khd->qhd", attend_low, values, preferred_element_type=jnp.float32)
        .reshape(token_count, inner_width)
        .astype(jnp.bfloat16)
    )
    output = floated + jnp.dot(mixed, proj_weight, preferred_element_type=jnp.float32)
    output_low = output.astype(jnp.bfloat16)
    logits = jnp.dot(output_low, head_weight, preferred_element_type=jnp.float32)
    logit_grad = LOSS_SCALE * (jax.nn.sigmoid(logits) - target.T.astype(jnp.float32))
    output_grad = jnp.dot(
        logit_grad, head_weight.astype(jnp.float32).T, precision=lax.Precision.HIGHEST
    )
    grad_low = output_grad.astype(jnp.bfloat16)
    proj_term = jnp.dot(mixed.T, grad_low, preferred_element_type=jnp.float32)
    mixed_grad = jnp.dot(grad_low, proj_weight.T, preferred_element_type=jnp.float32).astype(
        jnp.bfloat16
    )
    mixed_grad = mixed_grad.reshape(token_count, head_count, HEAD)
    value_grad = jnp.einsum(
        "hqk,qhd->khd", attend_low, mixed_grad, preferred_element_type=jnp.float32
    )
    attend_grad = jnp.einsum("qhd,khd->hqk", mixed_grad, values, preferred_element_type=jnp.float32)
    score_grad = (
        attend * (attend_grad - jnp.sum(attend_grad * attend, axis=-1, keepdims=True)) * score_scale
    )
    score_low = score_grad.astype(jnp.bfloat16)
    query_grad = jnp.einsum("hqk,khd->qhd", score_low, key_rows, preferred_element_type=jnp.float32)
    key_grad = jnp.einsum("hqk,qhd->khd", score_low, queries, preferred_element_type=jnp.float32)
    qkv_grad = jnp.concatenate(
        [
            query_grad.reshape(token_count, inner_width),
            key_grad.reshape(token_count, inner_width),
            value_grad.reshape(token_count, inner_width),
        ],
        axis=1,
    ).astype(jnp.bfloat16)
    qkv_term = jnp.dot(normed.T, qkv_grad, preferred_element_type=jnp.float32)
    normed_grad = jnp.dot(qkv_grad, qkv_weight.T, preferred_element_type=jnp.float32)
    grad_mean = jnp.mean(normed_grad, axis=-1, keepdims=True)
    grad_along = jnp.mean(normed_grad * unit_rows, axis=-1, keepdims=True)
    cell_grad = output_grad + inv_std * (normed_grad - grad_mean - unit_rows * grad_along)
    return (cell_grad.astype(jnp.bfloat16), qkv_term, proj_term)


def to_windows(grid):
    cells_x, cells_y, cells_z = (grid.shape[0], grid.shape[1], grid.shape[2])
    trailing = grid.shape[3:]
    shaped = grid.reshape(
        (cells_x // WIN, WIN, cells_y // WIN, WIN, cells_z // WIN, WIN) + trailing
    )
    order = (0, 2, 4, 1, 3, 5) + tuple(range(6, 6 + len(trailing)))
    return shaped.transpose(order).reshape((-1, WIN**3) + trailing)


def from_windows(windows, cells_x, cells_y, cells_z):
    width = windows.shape[-1]
    shaped = windows.reshape(cells_x // WIN, cells_y // WIN, cells_z // WIN, WIN, WIN, WIN, width)
    return shaped.transpose(0, 3, 1, 4, 2, 5, 6).reshape(cells_x, cells_y, cells_z, width)


def region_grid(cells_x, cells_y, cells_z):
    margin = WIN // 2
    whole_x = cells_x * lax.axis_size("gy")
    whole_y = cells_y * lax.axis_size("gx")
    coord_x = lax.axis_index("gy") * cells_x + jnp.arange(cells_x, dtype=jnp.int32)
    coord_y = lax.axis_index("gx") * cells_y + jnp.arange(cells_y, dtype=jnp.int32)
    coord_z = jnp.arange(cells_z, dtype=jnp.int32)
    flag_x = (coord_x >= whole_x - margin).astype(jnp.int32)
    flag_y = (coord_y >= whole_y - margin).astype(jnp.int32)
    flag_z = (coord_z >= cells_z - margin).astype(jnp.int32)
    return flag_x[:, None, None] * 4 + flag_y[None, :, None] * 2 + flag_z[None, None, :]


def slot_select(wanted, count):
    rank = jnp.cumsum(wanted.astype(jnp.int32)) - 1
    chosen = wanted[None, :] & (rank[None, :] == jnp.arange(count, dtype=jnp.int32)[:, None])
    return chosen.astype(jnp.bfloat16)


def per_device(volume, affinity, window_dest, qkv_weight, proj_weight, head_weight):
    margin = WIN // 2
    cells_x, cells_y, cells_z, width = (
        volume.shape[1],
        volume.shape[2],
        volume.shape[3],
        volume.shape[4],
    )
    cells = WIN**3
    rim_first, rim_first_aff = passed_along((volume[:, :margin], affinity[:, :, :margin]), "gy", -1)
    grown = jnp.concatenate([volume[:, margin:], rim_first], axis=1)
    grown_aff = jnp.concatenate([affinity[:, :, margin:], rim_first_aff], axis=2)
    rim_second, rim_second_aff = passed_along(
        (grown[:, :, :margin], grown_aff[:, :, :, :margin]), "gx", -1
    )
    grown = jnp.concatenate([grown[:, :, margin:], rim_second], axis=2)
    grown_aff = jnp.concatenate([grown_aff[:, :, :, margin:], rim_second_aff], axis=3)
    grown = jnp.roll(grown[0], -margin, axis=2)
    grown_aff = jnp.roll(grown_aff[0], -margin, axis=3)
    tokens = to_windows(grown)
    targets = jnp.moveaxis(to_windows(jnp.moveaxis(grown_aff, 0, -1)), -1, 1)
    regions = to_windows(region_grid(cells_x, cells_y, cells_z))
    destinations = window_dest.reshape(-1)
    window_count = destinations.shape[0]
    group_size = lax.axis_size("ga")
    balance_count = window_count // 2
    zero_qkv = jnp.zeros(qkv_weight.shape, jnp.float32)
    zero_proj = jnp.zeros(proj_weight.shape, jnp.float32)

    def step(carry, item):
        cell_grad, qkv_term, proj_term = window_grads(
            item[0], item[1], item[2], qkv_weight, proj_weight, head_weight
        )
        return ((carry[0] + qkv_term, carry[1] + proj_term), cell_grad)

    slots = window_count // 4
    reach = min(HOPS, group_size - 1)
    own = lax.axis_index("ga")
    relative = jnp.where(destinations < group_size, (destinations - own) % group_size, -1)
    region_low = (regions + 1).astype(jnp.bfloat16)

    def pack(select_low):
        packed_tokens = jnp.einsum(
            "sw,wtd->std", select_low, tokens, preferred_element_type=jnp.float32
        ).astype(jnp.bfloat16)
        packed_targets = jnp.einsum(
            "sw,wat->sat", select_low, targets, preferred_element_type=jnp.float32
        ).astype(jnp.bfloat16)
        packed_regions = (
            jnp.einsum("sw,wt->st", select_low, region_low, preferred_element_type=jnp.float32)
            - 1.0
        ).astype(jnp.bfloat16)
        return (packed_tokens, packed_targets, packed_regions)

    kept_select = slot_select(relative == 0, balance_count)
    gathered = [pack(kept_select)]
    selects = []
    for offset in range(1, reach + 1):
        moved_select = slot_select(relative == offset, slots)
        selects.append(moved_select)
        gathered.append(passed_along(for_sending(pack(moved_select)), "ga", offset))
    got_tokens = jnp.concatenate([item[0] for item in gathered], axis=0)
    got_targets = jnp.concatenate([item[1] for item in gathered], axis=0)
    got_regions = jnp.concatenate([item[2] for item in gathered], axis=0)
    filled = got_regions[:, 0].astype(jnp.float32) >= 0.0
    filled_rank = jnp.cumsum(filled.astype(jnp.int32)) - 1
    pick = filled[None, :] & (
        filled_rank[None, :] == jnp.arange(balance_count, dtype=jnp.int32)[:, None]
    )
    pick_low = pick.astype(jnp.bfloat16)
    work_tokens = jnp.einsum(
        "bs,std->btd", pick_low, got_tokens, preferred_element_type=jnp.float32
    ).astype(jnp.bfloat16)
    work_targets = jnp.einsum(
        "bs,sat->bat", pick_low, got_targets, preferred_element_type=jnp.float32
    ).astype(jnp.bfloat16)
    work_regions = jnp.einsum(
        "bs,st->bt", pick_low, got_regions, preferred_element_type=jnp.float32
    ).astype(jnp.int32)
    (total_qkv, total_proj), work_grads = lax.scan(
        step, (zero_qkv, zero_proj), (work_tokens, work_targets, work_regions)
    )
    send_back = jnp.einsum(
        "bs,btd->std", pick_low, work_grads, preferred_element_type=jnp.float32
    ).astype(jnp.bfloat16)
    gathered_grad = jnp.einsum(
        "sw,std->wtd", kept_select, send_back[:balance_count], preferred_element_type=jnp.float32
    )
    for offset in range(1, reach + 1):
        begin = balance_count + (offset - 1) * slots
        returned = passed_along(send_back[begin : begin + slots], "ga", -offset)
        gathered_grad = gathered_grad + jnp.einsum(
            "sw,std->wtd", selects[offset - 1], returned, preferred_element_type=jnp.float32
        )
    window_grad = gathered_grad.astype(jnp.bfloat16)
    grid_grad = from_windows(window_grad, cells_x, cells_y, cells_z)
    grid_grad = jnp.roll(grid_grad, margin, axis=2)
    back_second = passed_along(grid_grad[:, cells_y - margin :], "gx", 1)
    grid_grad = jnp.concatenate([back_second, grid_grad[:, : cells_y - margin]], axis=1)
    back_first = passed_along(grid_grad[cells_x - margin :], "gy", 1)
    grid_grad = jnp.concatenate([back_first, grid_grad[: cells_x - margin]], axis=0)
    share_qkv, share_proj = (
        lax.psum_scatter(total_qkv, "ga", scatter_dimension=0, tiled=True),
        lax.psum_scatter(total_proj, "ga", scatter_dimension=1, tiled=True),
    )
    summed_qkv, summed_proj = lax.psum((share_qkv, share_proj), ("gy", "gx"))
    live_cells = lax.axis_size("gy") * lax.axis_size("gx") * group_size * balance_count * cells
    factor = float(live_cells) ** (-0.5)
    return (grid_grad[None], summed_qkv * factor, summed_proj * factor)


def solution(mesh):
    placed = (
        P("ga", "gy", "gx", None, None),
        P("ga", None, "gy", "gx", None),
        P("ga", "gy", "gx", None),
        P(),
        P(),
        P(),
    )
    return jax.shard_map(
        per_device,
        mesh=mesh,
        in_specs=placed,
        out_specs=(P("ga", "gy", "gx", None, None), P("ga", None), P(None, "ga")),
        check_vma=False,
    )
```

profile of v0, /device:TPU:2, one launch (start us, length us, event | category | flops | bytes accessed | tf_op | source)
XLA Modules:
  0.0 543.5 jit_solution(7793813690417377618)
XLA Ops:
  22.0 8.0 %collective-permute-done.6 = bf16[1,3,3,14,7]{3,4,2,1,0:T(8,128)(2,1)S(1)} collective-permute-done((bf16[1,3,3,14,7]{3,4,2,1,0:T(8,128)(2,1)S(1)}, bf16[1,3,3,14,7]{3,4,2,1,0:T(8,128)(2,1)S(1)}, u32[]{:S(2)}, u32[]{:S(2)}) %collective-permute-start.6) | collective-permute-done | bytes 1796 | tf_op jit(solution)/shard_map/ppermute | solution.py:16
  30.1 4.6 collective-permute-start.7
  34.8 4.4 collective-permute-done.7
  41.6 4.6 collective-permute-start.3
  48.6 18.0 %collective-permute-done.3 = bf16[1,14,3,7,768]{4,3,2,1,0:T(8,128)(2,1)S(1)} collective-permute-done((bf16[1,14,3,7,768]{4,3,2,1,0:T(8,128)(2,1)S(1)}, bf16[1,14,3,7,768]{4,3,2,1,0:T(8,128)(2,1)S(1)}, u32[]{:S(2)}, u32[]{:S(2)}) %collective-permute-start.3) | collective-permute-done | bytes 451616 | tf_op jit(solution)/shard_map/ppermute | solution.py:16
  80.6 12.6 %collective-permute-done.4 = bf16[1,343,768]{2,1,0:T(8,128)(2,1)S(1)} collective-permute-done((bf16[1,343,768]{2,1,0:T(8,128)(2,1)S(1)}, bf16[1,343,768]{2,1,0:T(8,128)(2,1)S(1)}, u32[]{:S(2)}, u32[]{:S(2)}) %collective-permute-start.4) | collective-permute-done | bytes 526880 | tf_op jit(solution)/shard_map/ppermute | solution.py:16
  99.9 119.4 %while.15 = (s32[]{:T(128)}, f32[768,1152]{1,0:T(8,128)}, f32[384,768]{1,0:T(8,128)S(1)}, bf16[2,343,768]{2,1,0:T(8,128)(2,1)}, bf16[2,343,768]{2,1,0:T(8,128)(2...) while((s32[]{:T(128)}, f32[768,1152]{1,0:T(8,128)}, ...), condition=%wide.region_12.13_spmd.clone, body=%wide.region_4.12_spmd.clone.sunk | while | flops 3029209600 | bytes 97110760 | solution.py:207
  104.6 6.1 %fusion.227 = (f32[12,343]{1,0:T(8,128)S(1)}, f32[12,343,343]{1,2,0:T(8,128)}) fusion(pred[343,343]{0,1:T(8,128)(4,1)S(1)} %broadcast_compare_fusion.4, bf16[343,12,32]{0,2,1:T(8,128)(2,1)S(1)} %bitcast.327, bf16[343,12,32]{0,2,1:T(8,128)(2,1)} %bitcast.329), kind=kOutput, calls=%fused_computation.202.clone.1 | convolution fusion | flops 96001928 | bytes 6308113 | tf_op jit(solution)/shard_map/while/body/eval_jaxpr/sub | solution.py:46
  120.8 5.0 fusion.232
  125.8 10.9 %fusion.234 = bf16[12,32,343]{2,1,0:T(8,128)(2,1)} fusion(bf16[343,12,32]{0,2,1:T(8,128)(2,1)} %bitcast.330, f32[12,343,343]{1,2,0:T(8,128)} %fusion.232, f32[12,343,343]{1,2,0:T(8,128)} %get-tuple-element.243, f32[12,343]{1,0:T(8,128)S(1)} %get-tuple-element.244), kind=kOutput, calls=%fused_computation.32.clone.1 | convolution fusion | flops 100373120 | bytes 11837616 | tf_op jit(solution)/shard_map/while/body/eval_jaxpr/hqk,khd->qhd/dot_general | solution.py:75
  136.7 11.0 %fusion.233 = bf16[12,32,343]{2,1,0:T(8,128)(2,1)} fusion(bf16[343,12,32]{0,2,1:T(8,128)(2,1)} %bitcast.328, f32[12,343,343]{1,2,0:T(8,128)} %fusion.232, f32[12,343,343]{1,2,0:T(8,128)} %get-tuple-element.243, f32[12,343]{1,0:T(8,128)S(1)} %get-tuple-element.244), kind=kOutput, calls=%fused_computation.33.clone.1 | convolution fusion | flops 100373120 | bytes 11837616 | tf_op jit(solution)/shard_map/while/body/eval_jaxpr/hqk,qhd->khd/dot_general | solution.py:76
  163.5 6.1 %fusion.227 = (f32[12,343]{1,0:T(8,128)S(1)}, f32[12,343,343]{1,2,0:T(8,128)}) fusion(pred[343,343]{0,1:T(8,128)(4,1)S(1)} %broadcast_compare_fusion.4, bf16[343,12,32]{0,2,1:T(8,128)(2,1)S(1)} %bitcast.327, bf16[343,12,32]{0,2,1:T(8,128)(2,1)} %bitcast.329), kind=kOutput, calls=%fused_computation.202.clone.1 | convolution fusion | flops 96001928 | bytes 6308113 | tf_op jit(solution)/shard_map/while/body/eval_jaxpr/sub | solution.py:46
  179.7 5.0 fusion.232
  184.7 10.9 %fusion.234 = bf16[12,32,343]{2,1,0:T(8,128)(2,1)} fusion(bf16[343,12,32]{0,2,1:T(8,128)(2,1)} %bitcast.330, f32[12,343,343]{1,2,0:T(8,128)} %fusion.232, f32[12,343,343]{1,2,0:T(8,128)} %get-tuple-element.243, f32[12,343]{1,0:T(8,128)S(1)} %get-tuple-element.244), kind=kOutput, calls=%fused_computation.32.clone.1 | convolution fusion | flops 100373120 | bytes 11837616 | tf_op jit(solution)/shard_map/while/body/eval_jaxpr/hqk,khd->qhd/dot_general | solution.py:75
  195.6 11.0 %fusion.233 = bf16[12,32,343]{2,1,0:T(8,128)(2,1)} fusion(bf16[343,12,32]{0,2,1:T(8,128)(2,1)} %bitcast.328, f32[12,343,343]{1,2,0:T(8,128)} %fusion.232, f32[12,343,343]{1,2,0:T(8,128)} %get-tuple-element.243, f32[12,343]{1,0:T(8,128)S(1)} %get-tuple-element.244), kind=kOutput, calls=%fused_computation.33.clone.1 | convolution fusion | flops 100373120 | bytes 11837616 | tf_op jit(solution)/shard_map/while/body/eval_jaxpr/hqk,qhd->khd/dot_general | solution.py:76
  213.0 5.4 %convolution_add_fusion.6 = f32[768,1152]{1,0:T(8,128)} fusion(f32[768,1152]{1,0:T(8,128)} %get-tuple-element.263, pred[]{:T(512)S(6)} %compare.25, bf16[343,384]{0,1:T(8,128)(2,1)} %bitcast.326, bf16[343,384]{0,1:T(8,128)(2,1)} %bitcast.323, bf16[343,384]{0,1:T(8,128)(2,1)} %bitcast.321, f32[343]{0:T(512)S(1)} %add_rsqrt_fusion.2, ...), kind=kOutput, calls=%fused_computation.8.clone.1 | convolution fusion | flops 612122880 | bytes 8400645 | tf_op jit(solution)/shard_map/while/body/eval_jaxpr/dot_general | solution.py:85
  226.8 5.7 %collective-permute-start.10 = (bf16[1,343,768]{2,1,0:T(8,128)(2,1)S(1)}, bf16[1,343,768]{2,1,0:T(8,128)(2,1)S(1)}, u32[]{:S(2)}, u32[]{:S(2)}) collective-permute-start(bf16[1,343,768]{2,1,0:T(8,128)(2,1)S(1)} %copy.74), channel_id=1, source_target_pairs={{1,0},{2,1},{3,2},{4,3},{5,4},{6,5},{7,6},{8,7},{9,8},{10,9},{11,1... | collective-permute-start | bytes 1580552 | tf_op jit(solution)/shard_map/ppermute | solution.py:16
  232.5 5.2 collective-permute-done.11
  237.8 9.8 %collective-permute-done.10 = bf16[1,343,768]{2,1,0:T(8,128)(2,1)S(1)} collective-permute-done((bf16[1,343,768]{2,1,0:T(8,128)(2,1)S(1)}, bf16[1,343,768]{2,1,0:T(8,128)(2,1)S(1)}, u32[]{:S(2)}, u32[]{:S(2)}) %collective-permute-start.10) | collective-permute-done | bytes 526880 | tf_op jit(solution)/shard_map/ppermute | solution.py:16
  247.6 4.5 add_convert_fusion
  260.3 26.7 %collective-permute-done.12 = bf16[14,3,7,768]{3,2,1,0:T(8,128)(2,1)S(1)} collective-permute-done((bf16[14,3,7,768]{3,2,1,0:T(8,128)(2,1)S(1)}, bf16[14,3,7,768]{3,2,1,0:T(8,128)(2,1)S(1)}, u32[]{:S(2)}, u32[]{:S(2)}) %collective-permute-start.12) | collective-permute-done | bytes 451616 | tf_op jit(solution)/shard_map/ppermute | solution.py:16
  288.8 11.0 %reduce-scatter.5.cloned.1.call-done = f32[384,48]{0,1:T(8,128)} async-done(((f32[384,768]{0,1:T(8,128)}), f32[384,48]{0,1:T(8,128)}) %reduce-scatter.5.cloned.1.call-update) | async-done | bytes 73744 | tf_op jit(solution)/shard_map/reduce_scatter | solution.py:231
  299.8 72.3 %reduce-scatter.3.cloned.1.call-done = f32[48,1152]{1,0:T(8,128)} async-done(((f32[768,1152]{1,0:T(8,128)}), f32[48,1152]{1,0:T(8,128)}) %reduce-scatter.3.cloned.1.call-update) | async-done | bytes 221200 | tf_op jit(solution)/shard_map/reduce_scatter | solution.py:230
  375.5 158.1 %all-reduce.3.cloned.1.call-done = (f32[48,1152]{1,0:T(8,128)}, f32[384,48]{0,1:T(8,128)}) async-done(((f32[48,1152]{1,0:T(8,128)}, f32[384,48]{0,1:T(8,128)}), (f32[48,1152]{1,0:T(8,128)}, f32[384,48]{0,1:T(8,128)})) %all-reduce.3.cloned.1.call-update) | async-done | bytes 294928 | tf_op jit(solution)/shard_map/psum | solution.py:233
  (221 shorter events, 111.1 us)
Async XLA Ops:
  7.2 292.6 %reduce-scatter.5.cloned.1.call-start = ((), (), s32[]{:S(2)}) async-start(), calls=%async_computation.3 | async-start | bytes 1253376 | tf_op jit(solution)/shard_map/reduce_scatter | solution.py:231
  10.1 66.0 %copy-start.13 = (s32[1,1,1,4]{3,2,1,0:T(1,128)}, s32[1,1,1,4]{3,2,1,0:T(1,128)S(1)}, u32[]{:S(2)}) copy-start(s32[1,1,1,4]{3,2,1,0:T(1,128)S(1)} %get-tuple-element.148) | copy-start | bytes 52
  10.6 11.0 %collective-permute-start = (bf16[1,343]{1,0:T(2,128)(2,1)S(1)}, bf16[1,343]{1,0:T(2,128)(2,1)S(1)}, u32[]{:S(2)}, u32[]{:S(2)}) collective-permute-start(bf16[1,343]{1,0:T(2,128)(2,1)S(1)} %convert_element_type.190), channel_id=1, source_target_pairs={{15,0},{0,1},{1,2},{2,3},{3,4},{4,5},{5,6},{6,7},{7,8},{8,9},{9,10... | collective-permute-start | bytes 2066 | tf_op jit(solution)/shard_map/ppermute | solution.py:16
  10.9 65.2 %copy-start.15 = (pred[4]{0:T(512)(128)(4,1)}, pred[4]{0:T(512)(128)(4,1)S(1)}, u32[]{:S(2)}) copy-start(pred[4]{0:T(512)(128)(4,1)S(1)} %fusion.100) | copy-start | bytes 16
  11.0 10.6 %collective-permute-start.1 = (bf16[1,343]{1,0:T(2,128)(2,1)S(1)}, bf16[1,343]{1,0:T(2,128)(2,1)S(1)}, u32[]{:S(2)}, u32[]{:S(2)}) collective-permute-start(bf16[1,343]{1,0:T(2,128)(2,1)S(1)} %convert_element_type.193), channel_id=1, source_target_pairs={{14,0},{15,1},{0,2},{1,3},{2,4},{3,5},{4,6},{5,7},{6,8},{7,9},{8,1... | collective-permute-start | bytes 2066 | tf_op jit(solution)/shard_map/ppermute | solution.py:16
  14.9 25.8 %collective-permute-start.2 = (bf16[1,3,14,7,768]{4,3,2,1,0:T(8,128)(2,1)}, bf16[1,3,14,7,768]{4,3,2,1,0:T(8,128)(2,1)}, u32[]{:S(2)}, u32[]{:S(2)}) collective-permute-start(bf16[1,3,14,7,768]{4,3,2,1,0:T(8,128)(2,1)} %slice.83), channel_id=1, source_target_pairs={{64,0},{128,64},{192,128},{0,192},{65,1},{129,65},{193,129},{1,193... | collective-permute-start | bytes 1354760 | tf_op jit(solution)/shard_map/ppermute | solution.py:16
  16.1 13.9 %collective-permute-start.6 = (bf16[1,3,3,14,7]{3,4,2,1,0:T(8,128)(2,1)S(1)}, bf16[1,3,3,14,7]{3,4,2,1,0:T(8,128)(2,1)S(1)}, u32[]{:S(2)}, u32[]{:S(2)}) collective-permute-start(bf16[1,3,3,14,7]{3,4,2,1,0:T(8,128)(2,1)S(1)} %slice.89), channel_id=1, source_target_pairs={{64,0},{128,64},{192,128},{0,192},{65,1},{129,65},{193,129},{1,193... | collective-permute-start | bytes 5300 | tf_op jit(solution)/shard_map/ppermute | solution.py:16
  19.7 59.6 %copy-start.18 = (pred[2,4]{1,0:T(4,128)(4,1)}, pred[2,4]{1,0:T(4,128)(4,1)S(1)}, u32[]{:S(2)}) copy-start(pred[2,4]{1,0:T(4,128)(4,1)S(1)} %compare_and_fusion.1) | copy-start | bytes 28
  21.9 73.6 %copy-start.20 = (pred[2,4]{1,0:T(4,128)(4,1)}, pred[2,4]{1,0:T(4,128)(4,1)S(1)}, u32[]{:S(2)}) copy-start(pred[2,4]{1,0:T(4,128)(4,1)S(1)} %compare_and_fusion) | copy-start | bytes 28
  30.1 9.2 %collective-permute-start.7 = (bf16[1,3,14,3,7]{3,4,2,1,0:T(8,128)(2,1)S(1)}, bf16[1,3,14,3,7]{3,4,2,1,0:T(8,128)(2,1)S(1)}, u32[]{:S(2)}, u32[]{:S(2)}) collective-permute-start(bf16[1,3,14,3,7]{3,4,2,1,0:T(8,128)(2,1)S(1)} %pad_maximum_fusion.13), channel_id=1, source_target_pairs={{16,0},{32,16},{48,32},{0,48},{17,1},{33,17},{49,33},{1,49},{18,2}... | collective-permute-start | bytes 5300 | tf_op jit(solution)/shard_map/ppermute | solution.py:16
  41.6 24.9 %collective-permute-start.3 = (bf16[1,14,3,7,768]{4,3,2,1,0:T(8,128)(2,1)S(1)}, bf16[1,14,3,7,768]{4,3,2,1,0:T(8,128)(2,1)S(1)}, u32[]{:S(2)}, u32[]{:S(2)}) collective-permute-start(bf16[1,14,3,7,768]{4,3,2,1,0:T(8,128)(2,1)S(1)} %pad_maximum_fusion.12), channel_id=1, source_target_pairs={{16,0},{32,16},{48,32},{0,48},{17,1},{33,17},{49,33},{1,49},{18,2}... | collective-permute-start | bytes 1354760 | tf_op jit(solution)/shard_map/ppermute | solution.py:16
  46.4 32.8 %collective-permute-start.8 = (bf16[1,3,343]{2,0,1:T(2,128)(2,1)S(1)}, bf16[1,3,343]{2,0,1:T(2,128)(2,1)S(1)}, u32[]{:S(2)}, u32[]{:S(2)}) collective-permute-start(bf16[1,3,343]{2,0,1:T(2,128)(2,1)S(1)} %copy.69), channel_id=1, source_target_pairs={{15,0},{0,1},{1,2},{2,3},{3,4},{4,5},{5,6},{6,7},{7,8},{8,9},{9,10... | collective-permute-start | bytes 6182 | tf_op jit(solution)/shard_map/ppermute | solution.py:16
  46.5 32.6 %collective-permute-start.9 = (bf16[1,3,343]{2,0,1:T(2,128)(2,1)S(1)}, bf16[1,3,343]{2,0,1:T(2,128)(2,1)S(1)}, u32[]{:S(2)}, u32[]{:S(2)}) collective-permute-start(bf16[1,3,343]{2,0,1:T(2,128)(2,1)S(1)} %copy.70), channel_id=1, source_target_pairs={{14,0},{15,1},{0,2},{1,3},{2,4},{3,5},{4,6},{5,7},{6,8},{7,9},{8,1... | collective-permute-start | bytes 6182 | tf_op jit(solution)/shard_map/ppermute | solution.py:16
  77.4 15.8 %collective-permute-start.4 = (bf16[1,343,768]{2,1,0:T(8,128)(2,1)S(1)}, bf16[1,343,768]{2,1,0:T(8,128)(2,1)S(1)}, u32[]{:S(2)}, u32[]{:S(2)}) collective-permute-start(bf16[1,343,768]{2,1,0:T(8,128)(2,1)S(1)} %copy.102), channel_id=1, source_target_pairs={{15,0},{0,1},{1,2},{2,3},{3,4},{4,5},{5,6},{6,7},{7,8},{8,9},{9,10... | collective-permute-start | bytes 1580552 | tf_op jit(solution)/shard_map/ppermute | solution.py:16
  77.6 17.1 %collective-permute-start.5 = (bf16[1,343,768]{2,1,0:T(8,128)(2,1)S(1)}, bf16[1,343,768]{2,1,0:T(8,128)(2,1)S(1)}, u32[]{:S(2)}, u32[]{:S(2)}) collective-permute-start(bf16[1,343,768]{2,1,0:T(8,128)(2,1)S(1)} %copy.103), channel_id=1, source_target_pairs={{14,0},{15,1},{0,2},{1,3},{2,4},{3,5},{4,6},{5,7},{6,8},{7,9},{8,1... | collective-permute-start | bytes 1580552 | tf_op jit(solution)/shard_map/ppermute | solution.py:16
  220.8 151.2 %reduce-scatter.3.cloned.1.call-start = ((), (), s32[]{:S(2)}) async-start(), calls=%async_computation.2 | async-start | bytes 3760128 | tf_op jit(solution)/shard_map/reduce_scatter | solution.py:230
  221.6 312.0 %all-reduce.3.cloned.1.call-start = ((), (), s32[]{:S(2)}) async-start(), calls=%async_computation.4 | async-start | bytes 589824 | tf_op jit(solution)/shard_map/psum | solution.py:233
  226.5 11.2 %collective-permute-start.11 = (bf16[1,343,768]{2,1,0:T(8,128)(2,1)S(1)}, bf16[1,343,768]{2,1,0:T(8,128)(2,1)S(1)}, u32[]{:S(2)}, u32[]{:S(2)}) collective-permute-start(bf16[1,343,768]{2,1,0:T(8,128)(2,1)S(1)} %copy.75), channel_id=1, source_target_pairs={{2,0},{3,1},{4,2},{5,3},{6,4},{7,5},{8,6},{9,7},{10,8},{11,9},{12,... | collective-permute-start | bytes 1580552 | tf_op jit(solution)/shard_map/ppermute | solution.py:16
  226.8 20.8 %copy-start.12 = (f32[4]{0:T(128)S(1)}, f32[4]{0:T(128)}, u32[]{:S(2)}) copy-start(f32[4]{0:T(128)} %get-tuple-element.147) | copy-start | bytes 52
  226.8 20.8 %copy-start.19 = (pred[2,4]{1,0:T(4,128)(4,1)S(1)}, pred[2,4]{1,0:T(4,128)(4,1)}, u32[]{:S(2)}) copy-start(pred[2,4]{1,0:T(4,128)(4,1)} %copy-done.18) | copy-start | bytes 28
  226.8 20.7 %collective-permute-start.10 = (bf16[1,343,768]{2,1,0:T(8,128)(2,1)S(1)}, bf16[1,343,768]{2,1,0:T(8,128)(2,1)S(1)}, u32[]{:S(2)}, u32[]{:S(2)}) collective-permute-start(bf16[1,343,768]{2,1,0:T(8,128)(2,1)S(1)} %copy.74), channel_id=1, source_target_pairs={{1,0},{2,1},{3,2},{4,3},{5,4},{6,5},{7,6},{8,7},{9,8},{10,9},{11,1... | collective-permute-start | bytes 1580552 | tf_op jit(solution)/shard_map/ppermute | solution.py:16
  257.8 29.4 %copy-start.1 = (bf16[14,14,4,768]{3,2,1,0:T(4,128)(2,1)}, bf16[14,14,4,768]{3,2,1,0:T(4,128)(2,1)S(1)}, u32[]{:S(2)}) copy-start(bf16[14,14,4,768]{3,2,1,0:T(4,128)(2,1)S(1)} %slice.121) | copy-start | bytes 3612676
  258.1 28.9 %collective-permute-start.12 = (bf16[14,3,7,768]{3,2,1,0:T(8,128)(2,1)S(1)}, bf16[14,3,7,768]{3,2,1,0:T(8,128)(2,1)S(1)}, u32[]{:S(2)}, u32[]{:S(2)}) collective-permute-start(bf16[14,3,7,768]{3,2,1,0:T(8,128)(2,1)S(1)} %pad_maximum_fusion.11), channel_id=1, source_target_pairs={{48,0},{0,16},{16,32},{32,48},{49,1},{1,17},{17,33},{33,49},{50,2}... | collective-permute-start | bytes 1354760 | tf_op jit(solution)/shard_map/ppermute | solution.py:16
  287.2 84.9 %collective-permute-start.13 = (bf16[3,14,7,768]{3,2,1,0:T(8,128)(2,1)S(1)}, bf16[3,14,7,768]{3,2,1,0:T(8,128)(2,1)S(1)}, u32[]{:S(2)}, u32[]{:S(2)}) collective-permute-start(bf16[3,14,7,768]{3,2,1,0:T(8,128)(2,1)S(1)} %pad_maximum_fusion.10), channel_id=1, source_target_pairs={{192,0},{0,64},{64,128},{128,192},{193,1},{1,65},{65,129},{129,193... | collective-permute-start | bytes 1354760 | tf_op jit(solution)/shard_map/ppermute | solution.py:16
  (24 other events, 86.7 us)
Sparse Core Ops, SparseCore 0:
  220.9 78.7 reduce-scatter.4
  302.3 69.7 reduce-scatter.2
  374.8 158.7 all-reduce.2
where the time goes:
time: 550 us; the launch traced here: 543 us
  waiting for transfers between devices  327 us (59%)
  matrix products  124 us (23%)
  local copies, waits for them, and re-layouts  30.1 us (5%)
  starting transfers between devices  26.7 us (5%)
  other arithmetic  19.4 us (4%)
  between operations  14.5 us (3%)
    psum x1, waiting for transfers between devices, per_device(): summed_qkv, summed_proj = lax.psum((share_qkv, share_proj), ('gy', 'gx'))  158 us
    ppermute x14, waiting for transfers between devices, passed_along(): return lax.ppermute(block, axis, route)  85.3 us
    reduce_scatter x1, waiting for transfers between devices, per_device(): lax.psum_scatter(total_qkv, 'ga', scatter_dimension=0, tiled=True)  72.3 us
    ppermute x14, starting transfers between devices, passed_along(): return lax.ppermute(block, axis, route)  26.6 us
    dot_general x2, matrix products, window_grads(): jnp.einsum('hqk,qhd->khd', score_low, queries, preferred_element_type=jnp...  21.9 us
    dot_general x2, matrix products, window_grads(): jnp.einsum('hqk,khd->qhd', score_low, key_rows, preferred_element_type=jn...  21.8 us
    sub x2, matrix products, window_grads(): exponent = jnp.exp(scores - row_max)  12.3 us
  transfers between devices with their start and end apart: 17, of which 11 were waited for; matrix products, arithmetic and copies ran while one was open for 8% of the time, Pallas kernels for 0%

commit v1 on v0

--- a/solution.py
+++ b/solution.py
@@ -8,6 +8,12 @@
 HOPS = 2
 LOSS_SCALE = 32.0
 EPSILON = 1e-05
+
+
+def refer_results_for(mesh_dim, axis_name, xin):
+    for tick in (mesh_dim, axis_name):
+        xin = lax.psum(xin, tick)
+    return xin
 
 
 def passed_along(block, axis, distance):
@@ -230,7 +236,7 @@
         lax.psum_scatter(total_qkv, "ga", scatter_dimension=0, tiled=True),
         lax.psum_scatter(total_proj, "ga", scatter_dimension=1, tiled=True),
     )
-    summed_qkv, summed_proj = lax.psum((share_qkv, share_proj), ("gy", "gx"))
+    summed_qkv, summed_proj = refer_results_for("gy", "gx", (share_qkv, share_proj))
     live_cells = lax.axis_size("gy") * lax.axis_size("gx") * group_size * balance_count * cells
     factor = float(live_cells) ** (-0.5)
     return (grid_grad[None], summed_qkv * factor, summed_proj * factor)

time: 550 us -> 491 us (0.89)
  waiting for transfers between devices: 327 us -> 269 us
    psum x1 -> x2, waiting for transfers between devices: 158 us -> 100 us  [refer_results_for(): xin = lax.psum(xin, tick)]
  transfers between devices with their start and end apart: 17 -> 18, of which waited for: 11 -> 12; matrix products, arithmetic and copies ran while one was open for 8% -> 8% of each run, Pallas kernels for 0% -> 0%
where the time goes in v1:
time: 491 us; the launch traced here: 484 us
  waiting for transfers between devices  269 us (55%)
  matrix products  124 us (25%)
  local copies, waits for them, and re-layouts  30.1 us (6%)
  starting transfers between devices  26.7 us (5%)
  other arithmetic  19.1 us (4%)
  between operations  14.5 us (3%)
    psum x2, waiting for transfers between devices, refer_results_for(): xin = lax.psum(xin, tick)  100 us
    ppermute x14, waiting for transfers between devices, passed_along(): return lax.ppermute(block, axis, route)  85.3 us
    reduce_scatter x1, waiting for transfers between devices, per_device(): lax.psum_scatter(total_qkv, 'ga', scatter_dimension=0, tiled=True)  72.3 us
    ppermute x14, starting transfers between devices, passed_along(): return lax.ppermute(block, axis, route)  26.5 us
    dot_general x2, matrix products, window_grads(): jnp.einsum('hqk,qhd->khd', score_low, queries, preferred_element_type=jnp...  21.9 us
    dot_general x2, matrix products, window_grads(): jnp.einsum('hqk,khd->qhd', score_low, key_rows, preferred_element_type=jn...  21.8 us
    sub x2, matrix products, window_grads(): exponent = jnp.exp(scores - row_max)  12.3 us
    reduce_scatter x1, waiting for transfers between devices, per_device(): lax.psum_scatter(total_proj, 'ga', scatter_dimension=1, tiled=True)  10.2 us
  transfers between devices with their start and end apart: 18, of which 12 were waited for; matrix products, arithmetic and copies ran while one was open for 8% of the time, Pallas kernels for 0%

profile of v1, /device:TPU:2, one launch (start us, length us, event | category | flops | bytes accessed | tf_op | source)
XLA Modules:
  0.0 484.5 jit_solution(4621568000613979231)
XLA Ops:
  22.0 8.0 %collective-permute-done.6 = bf16[1,3,3,14,7]{3,4,2,1,0:T(8,128)(2,1)S(1)} collective-permute-done((bf16[1,3,3,14,7]{3,4,2,1,0:T(8,128)(2,1)S(1)}, bf16[1,3,3,14,7]{3,4,2,1,0:T(8,128)(2,1)S(1)}, u32[]{:S(2)}, u32[]{:S(2)}) %collective-permute-start.6) | collective-permute-done | bytes 1796 | tf_op jit(solution)/shard_map/ppermute | solution.py:22
  30.1 4.6 collective-permute-start.7
  41.6 4.6 collective-permute-start.3
  48.6 18.0 %collective-permute-done.3 = bf16[1,14,3,7,768]{4,3,2,1,0:T(8,128)(2,1)S(1)} collective-permute-done((bf16[1,14,3,7,768]{4,3,2,1,0:T(8,128)(2,1)S(1)}, bf16[1,14,3,7,768]{4,3,2,1,0:T(8,128)(2,1)S(1)}, u32[]{:S(2)}, u32[]{:S(2)}) %collective-permute-start.3) | collective-permute-done | bytes 451616 | tf_op jit(solution)/shard_map/ppermute | solution.py:22
  80.6 12.6 %collective-permute-done.4 = bf16[1,343,768]{2,1,0:T(8,128)(2,1)S(1)} collective-permute-done((bf16[1,343,768]{2,1,0:T(8,128)(2,1)S(1)}, bf16[1,343,768]{2,1,0:T(8,128)(2,1)S(1)}, u32[]{:S(2)}, u32[]{:S(2)}) %collective-permute-start.4) | collective-permute-done | bytes 526880 | tf_op jit(solution)/shard_map/ppermute | solution.py:22
  99.9 119.4 %while.15 = (s32[]{:T(128)}, f32[768,1152]{1,0:T(8,128)}, f32[384,768]{1,0:T(8,128)S(1)}, bf16[2,343,768]{2,1,0:T(8,128)(2,1)}, bf16[2,343,768]{2,1,0:T(8,128)(2...) while((s32[]{:T(128)}, f32[768,1152]{1,0:T(8,128)}, ...), condition=%wide.region_12.13_spmd.clone, body=%wide.region_4.12_spmd.clone.sunk | while | flops 3029209600 | bytes 97110760 | solution.py:213
  104.6 6.1 %fusion.227 = (f32[12,343]{1,0:T(8,128)S(1)}, f32[12,343,343]{1,2,0:T(8,128)}) fusion(pred[343,343]{0,1:T(8,128)(4,1)S(1)} %broadcast_compare_fusion.4, bf16[343,12,32]{0,2,1:T(8,128)(2,1)S(1)} %bitcast.327, bf16[343,12,32]{0,2,1:T(8,128)(2,1)} %bitcast.329), kind=kOutput, calls=%fused_computation.202.clone.1 | convolution fusion | flops 96001928 | bytes 6308113 | tf_op jit(solution)/shard_map/while/body/eval_jaxpr/sub | solution.py:52
  120.8 5.0 %fusion.232 = f32[12,343,343]{1,2,0:T(8,128)} fusion(bf16[343,12,32]{0,2,1:T(8,128)(2,1)} %bitcast.312, bf16[343,12,32]{0,2,1:T(8,128)(2,1)} %bitcast.315), kind=kOutput, calls=%fused_computation.205.clone.1 | convolution fusion | flops 90354432 | bytes 6174000 | tf_op jit(solution)/shard_map/while/body/eval_jaxpr/qhd,khd->hqk/dot_general | solution.py:76
  125.8 10.9 %fusion.234 = bf16[12,32,343]{2,1,0:T(8,128)(2,1)} fusion(bf16[343,12,32]{0,2,1:T(8,128)(2,1)} %bitcast.330, f32[12,343,343]{1,2,0:T(8,128)} %fusion.232, f32[12,343,343]{1,2,0:T(8,128)} %get-tuple-element.245, f32[12,343]{1,0:T(8,128)S(1)} %get-tuple-element.246), kind=kOutput, calls=%fused_computation.32.clone.1 | convolution fusion | flops 100373120 | bytes 11837616 | tf_op jit(solution)/shard_map/while/body/eval_jaxpr/hqk,khd->qhd/dot_general | solution.py:81
  136.7 11.0 %fusion.233 = bf16[12,32,343]{2,1,0:T(8,128)(2,1)} fusion(bf16[343,12,32]{0,2,1:T(8,128)(2,1)} %bitcast.328, f32[12,343,343]{1,2,0:T(8,128)} %fusion.232, f32[12,343,343]{1,2,0:T(8,128)} %get-tuple-element.245, f32[12,343]{1,0:T(8,128)S(1)} %get-tuple-element.246), kind=kOutput, calls=%fused_computation.33.clone.1 | convolution fusion | flops 100373120 | bytes 11837616 | tf_op jit(solution)/shard_map/while/body/eval_jaxpr/hqk,qhd->khd/dot_general | solution.py:82
  163.5 6.1 %fusion.227 = (f32[12,343]{1,0:T(8,128)S(1)}, f32[12,343,343]{1,2,0:T(8,128)}) fusion(pred[343,343]{0,1:T(8,128)(4,1)S(1)} %broadcast_compare_fusion.4, bf16[343,12,32]{0,2,1:T(8,128)(2,1)S(1)} %bitcast.327, bf16[343,12,32]{0,2,1:T(8,128)(2,1)} %bitcast.329), kind=kOutput, calls=%fused_computation.202.clone.1 | convolution fusion | flops 96001928 | bytes 6308113 | tf_op jit(solution)/shard_map/while/body/eval_jaxpr/sub | solution.py:52
  179.7 5.0 %fusion.232 = f32[12,343,343]{1,2,0:T(8,128)} fusion(bf16[343,12,32]{0,2,1:T(8,128)(2,1)} %bitcast.312, bf16[343,12,32]{0,2,1:T(8,128)(2,1)} %bitcast.315), kind=kOutput, calls=%fused_computation.205.clone.1 | convolution fusion | flops 90354432 | bytes 6174000 | tf_op jit(solution)/shard_map/while/body/eval_jaxpr/qhd,khd->hqk/dot_general | solution.py:76
  184.7 10.9 %fusion.234 = bf16[12,32,343]{2,1,0:T(8,128)(2,1)} fusion(bf16[343,12,32]{0,2,1:T(8,128)(2,1)} %bitcast.330, f32[12,343,343]{1,2,0:T(8,128)} %fusion.232, f32[12,343,343]{1,2,0:T(8,128)} %get-tuple-element.245, f32[12,343]{1,0:T(8,128)S(1)} %get-tuple-element.246), kind=kOutput, calls=%fused_computation.32.clone.1 | convolution fusion | flops 100373120 | bytes 11837616 | tf_op jit(solution)/shard_map/while/body/eval_jaxpr/hqk,khd->qhd/dot_general | solution.py:81
  195.6 11.0 %fusion.233 = bf16[12,32,343]{2,1,0:T(8,128)(2,1)} fusion(bf16[343,12,32]{0,2,1:T(8,128)(2,1)} %bitcast.328, f32[12,343,343]{1,2,0:T(8,128)} %fusion.232, f32[12,343,343]{1,2,0:T(8,128)} %get-tuple-element.245, f32[12,343]{1,0:T(8,128)S(1)} %get-tuple-element.246), kind=kOutput, calls=%fused_computation.33.clone.1 | convolution fusion | flops 100373120 | bytes 11837616 | tf_op jit(solution)/shard_map/while/body/eval_jaxpr/hqk,qhd->khd/dot_general | solution.py:82
  213.0 5.4 %convolution_add_fusion.6 = f32[768,1152]{1,0:T(8,128)} fusion(f32[768,1152]{1,0:T(8,128)} %get-tuple-element.265, pred[]{:T(512)S(6)} %compare.25, bf16[343,384]{0,1:T(8,128)(2,1)} %bitcast.326, bf16[343,384]{0,1:T(8,128)(2,1)} %bitcast.323, bf16[343,384]{0,1:T(8,128)(2,1)} %bitcast.321, f32[343]{0:T(512)S(1)} %add_rsqrt_fusion.2, ...), kind=kOutput, calls=%fused_computation.8.clone.1 | convolution fusion | flops 612122880 | bytes 8400645 | tf_op jit(solution)/shard_map/while/body/eval_jaxpr/dot_general | solution.py:91
  226.7 5.7 %collective-permute-start.10 = (bf16[1,343,768]{2,1,0:T(8,128)(2,1)S(1)}, bf16[1,343,768]{2,1,0:T(8,128)(2,1)S(1)}, u32[]{:S(2)}, u32[]{:S(2)}) collective-permute-start(bf16[1,343,768]{2,1,0:T(8,128)(2,1)S(1)} %copy.74), channel_id=1, source_target_pairs={{1,0},{2,1},{3,2},{4,3},{5,4},{6,5},{7,6},{8,7},{9,8},{10,9},{11,1... | collective-permute-start | bytes 1580552 | tf_op jit(solution)/shard_map/ppermute | solution.py:22
  232.5 5.2 %collective-permute-done.11 = bf16[1,343,768]{2,1,0:T(8,128)(2,1)S(1)} collective-permute-done((bf16[1,343,768]{2,1,0:T(8,128)(2,1)S(1)}, bf16[1,343,768]{2,1,0:T(8,128)(2,1)S(1)}, u32[]{:S(2)}, u32[]{:S(2)}) %collective-permute-start.11) | collective-permute-done | bytes 526880 | tf_op jit(solution)/shard_map/ppermute | solution.py:22
  237.7 9.8 %collective-permute-done.10 = bf16[1,343,768]{2,1,0:T(8,128)(2,1)S(1)} collective-permute-done((bf16[1,343,768]{2,1,0:T(8,128)(2,1)S(1)}, bf16[1,343,768]{2,1,0:T(8,128)(2,1)S(1)}, u32[]{:S(2)}, u32[]{:S(2)}) %collective-permute-start.10) | collective-permute-done | bytes 526880 | tf_op jit(solution)/shard_map/ppermute | solution.py:22
  247.6 4.5 add_convert_fusion
  260.2 26.7 %collective-permute-done.12 = bf16[14,3,7,768]{3,2,1,0:T(8,128)(2,1)S(1)} collective-permute-done((bf16[14,3,7,768]{3,2,1,0:T(8,128)(2,1)S(1)}, bf16[14,3,7,768]{3,2,1,0:T(8,128)(2,1)S(1)}, u32[]{:S(2)}, u32[]{:S(2)}) %collective-permute-start.12) | collective-permute-done | bytes 451616 | tf_op jit(solution)/shard_map/ppermute | solution.py:22
  289.4 10.2 %reduce-scatter.5.cloned.1.call-done = f32[384,48]{0,1:T(8,128)} async-done(((f32[384,768]{0,1:T(8,128)}), f32[384,48]{0,1:T(8,128)}) %reduce-scatter.5.cloned.1.call-update) | async-done | bytes 73744 | tf_op jit(solution)/shard_map/reduce_scatter | solution.py:237
  299.6 72.3 %reduce-scatter.3.cloned.1.call-done = f32[48,1152]{1,0:T(8,128)} async-done(((f32[768,1152]{1,0:T(8,128)}), f32[48,1152]{1,0:T(8,128)}) %reduce-scatter.3.cloned.1.call-update) | async-done | bytes 221200 | tf_op jit(solution)/shard_map/reduce_scatter | solution.py:236
  372.0 46.8 %all-reduce.7.cloned.1.call-done = (f32[48,1152]{1,0:T(8,128)}, f32[384,48]{0,1:T(8,128)}) async-done(((f32[48,1152]{1,0:T(8,128)}, f32[384,48]{0,1:T(8,128)}), (f32[48,1152]{1,0:T(8,128)}, f32[384,48]{0,1:T(8,128)})) %all-reduce.7.cloned.1.call-update) | async-done | bytes 294928 | tf_op jit(solution)/shard_map/psum | solution.py:15
  421.1 53.5 %all-reduce.5.cloned.1.call-done = (f32[48,1152]{1,0:T(8,128)}, f32[384,48]{0,1:T(8,128)}) async-done(((f32[48,1152]{1,0:T(8,128)}, f32[384,48]{0,1:T(8,128)}), (f32[48,1152]{1,0:T(8,128)}, f32[384,48]{0,1:T(8,128)})) %all-reduce.5.cloned.1.call-update) | async-done | bytes 294928 | tf_op jit(solution)/shard_map/psum | solution.py:15
  (222 shorter events, 115.1 us)
Async XLA Ops:
  7.2 292.4 %reduce-scatter.5.cloned.1.call-start = ((), (), s32[]{:S(2)}) async-start(), calls=%async_computation.3 | async-start | bytes 1253376 | tf_op jit(solution)/shard_map/reduce_scatter | solution.py:237
  10.1 66.0 %copy-start.12 = (s32[1,1,1,4]{3,2,1,0:T(1,128)}, s32[1,1,1,4]{3,2,1,0:T(1,128)S(1)}, u32[]{:S(2)}) copy-start(s32[1,1,1,4]{3,2,1,0:T(1,128)S(1)} %get-tuple-element.150) | copy-start | bytes 52
  10.6 11.0 %collective-permute-start = (bf16[1,343]{1,0:T(2,128)(2,1)S(1)}, bf16[1,343]{1,0:T(2,128)(2,1)S(1)}, u32[]{:S(2)}, u32[]{:S(2)}) collective-permute-start(bf16[1,343]{1,0:T(2,128)(2,1)S(1)} %convert_element_type.190), channel_id=1, source_target_pairs={{15,0},{0,1},{1,2},{2,3},{3,4},{4,5},{5,6},{6,7},{7,8},{8,9},{9,10... | collective-permute-start | bytes 2066 | tf_op jit(solution)/shard_map/ppermute | solution.py:22
  10.9 65.2 %copy-start.14 = (pred[4]{0:T(512)(128)(4,1)}, pred[4]{0:T(512)(128)(4,1)S(1)}, u32[]{:S(2)}) copy-start(pred[4]{0:T(512)(128)(4,1)S(1)} %fusion.100) | copy-start | bytes 16
  11.0 10.6 %collective-permute-start.1 = (bf16[1,343]{1,0:T(2,128)(2,1)S(1)}, bf16[1,343]{1,0:T(2,128)(2,1)S(1)}, u32[]{:S(2)}, u32[]{:S(2)}) collective-permute-start(bf16[1,343]{1,0:T(2,128)(2,1)S(1)} %convert_element_type.193), channel_id=1, source_target_pairs={{14,0},{15,1},{0,2},{1,3},{2,4},{3,5},{4,6},{5,7},{6,8},{7,9},{8,1... | collective-permute-start | bytes 2066 | tf_op jit(solution)/shard_map/ppermute | solution.py:22
  14.9 25.8 %collective-permute-start.2 = (bf16[1,3,14,7,768]{4,3,2,1,0:T(8,128)(2,1)}, bf16[1,3,14,7,768]{4,3,2,1,0:T(8,128)(2,1)}, u32[]{:S(2)}, u32[]{:S(2)}) collective-permute-start(bf16[1,3,14,7,768]{4,3,2,1,0:T(8,128)(2,1)} %slice.83), channel_id=1, source_target_pairs={{64,0},{128,64},{192,128},{0,192},{65,1},{129,65},{193,129},{1,193... | collective-permute-start | bytes 1354760 | tf_op jit(solution)/shard_map/ppermute | solution.py:22
  16.1 13.9 %collective-permute-start.6 = (bf16[1,3,3,14,7]{3,4,2,1,0:T(8,128)(2,1)S(1)}, bf16[1,3,3,14,7]{3,4,2,1,0:T(8,128)(2,1)S(1)}, u32[]{:S(2)}, u32[]{:S(2)}) collective-permute-start(bf16[1,3,3,14,7]{3,4,2,1,0:T(8,128)(2,1)S(1)} %slice.89), channel_id=1, source_target_pairs={{64,0},{128,64},{192,128},{0,192},{65,1},{129,65},{193,129},{1,193... | collective-permute-start | bytes 5300 | tf_op jit(solution)/shard_map/ppermute | solution.py:22
  19.7 59.6 %copy-start.17 = (pred[2,4]{1,0:T(4,128)(4,1)}, pred[2,4]{1,0:T(4,128)(4,1)S(1)}, u32[]{:S(2)}) copy-start(pred[2,4]{1,0:T(4,128)(4,1)S(1)} %compare_and_fusion.1) | copy-start | bytes 28
  21.9 73.6 %copy-start.19 = (pred[2,4]{1,0:T(4,128)(4,1)}, pred[2,4]{1,0:T(4,128)(4,1)S(1)}, u32[]{:S(2)}) copy-start(pred[2,4]{1,0:T(4,128)(4,1)S(1)} %compare_and_fusion) | copy-start | bytes 28
  30.1 9.2 %collective-permute-start.7 = (bf16[1,3,14,3,7]{3,4,2,1,0:T(8,128)(2,1)S(1)}, bf16[1,3,14,3,7]{3,4,2,1,0:T(8,128)(2,1)S(1)}, u32[]{:S(2)}, u32[]{:S(2)}) collective-permute-start(bf16[1,3,14,3,7]{3,4,2,1,0:T(8,128)(2,1)S(1)} %pad_maximum_fusion.13), channel_id=1, source_target_pairs={{16,0},{32,16},{48,32},{0,48},{17,1},{33,17},{49,33},{1,49},{18,2}... | collective-permute-start | bytes 5300 | tf_op jit(solution)/shard_map/ppermute | solution.py:22
  41.6 24.9 %collective-permute-start.3 = (bf16[1,14,3,7,768]{4,3,2,1,0:T(8,128)(2,1)S(1)}, bf16[1,14,3,7,768]{4,3,2,1,0:T(8,128)(2,1)S(1)}, u32[]{:S(2)}, u32[]{:S(2)}) collective-permute-start(bf16[1,14,3,7,768]{4,3,2,1,0:T(8,128)(2,1)S(1)} %pad_maximum_fusion.12), channel_id=1, source_target_pairs={{16,0},{32,16},{48,32},{0,48},{17,1},{33,17},{49,33},{1,49},{18,2}... | collective-permute-start | bytes 1354760 | tf_op jit(solution)/shard_map/ppermute | solution.py:22
  46.4 32.8 %collective-permute-start.8 = (bf16[1,3,343]{2,0,1:T(2,128)(2,1)S(1)}, bf16[1,3,343]{2,0,1:T(2,128)(2,1)S(1)}, u32[]{:S(2)}, u32[]{:S(2)}) collective-permute-start(bf16[1,3,343]{2,0,1:T(2,128)(2,1)S(1)} %copy.69), channel_id=1, source_target_pairs={{15,0},{0,1},{1,2},{2,3},{3,4},{4,5},{5,6},{6,7},{7,8},{8,9},{9,10... | collective-permute-start | bytes 6182 | tf_op jit(solution)/shard_map/ppermute | solution.py:22
  46.5 32.6 %collective-permute-start.9 = (bf16[1,3,343]{2,0,1:T(2,128)(2,1)S(1)}, bf16[1,3,343]{2,0,1:T(2,128)(2,1)S(1)}, u32[]{:S(2)}, u32[]{:S(2)}) collective-permute-start(bf16[1,3,343]{2,0,1:T(2,128)(2,1)S(1)} %copy.70), channel_id=1, source_target_pairs={{14,0},{15,1},{0,2},{1,3},{2,4},{3,5},{4,6},{5,7},{6,8},{7,9},{8,1... | collective-permute-start | bytes 6182 | tf_op jit(solution)/shard_map/ppermute | solution.py:22
  77.4 15.8 %collective-permute-start.4 = (bf16[1,343,768]{2,1,0:T(8,128)(2,1)S(1)}, bf16[1,343,768]{2,1,0:T(8,128)(2,1)S(1)}, u32[]{:S(2)}, u32[]{:S(2)}) collective-permute-start(bf16[1,343,768]{2,1,0:T(8,128)(2,1)S(1)} %copy.102), channel_id=1, source_target_pairs={{15,0},{0,1},{1,2},{2,3},{3,4},{4,5},{5,6},{6,7},{7,8},{8,9},{9,10... | collective-permute-start | bytes 1580552 | tf_op jit(solution)/shard_map/ppermute | solution.py:22
  77.6 17.1 %collective-permute-start.5 = (bf16[1,343,768]{2,1,0:T(8,128)(2,1)S(1)}, bf16[1,343,768]{2,1,0:T(8,128)(2,1)S(1)}, u32[]{:S(2)}, u32[]{:S(2)}) collective-permute-start(bf16[1,343,768]{2,1,0:T(8,128)(2,1)S(1)} %copy.103), channel_id=1, source_target_pairs={{14,0},{15,1},{0,2},{1,3},{2,4},{3,5},{4,6},{5,7},{6,8},{7,9},{8,1... | collective-permute-start | bytes 1580552 | tf_op jit(solution)/shard_map/ppermute | solution.py:22
  220.8 151.1 %reduce-scatter.3.cloned.1.call-start = ((), (), s32[]{:S(2)}) async-start(), calls=%async_computation.2 | async-start | bytes 3760128 | tf_op jit(solution)/shard_map/reduce_scatter | solution.py:236
  221.5 197.2 %all-reduce.7.cloned.1.call-start = ((), (), s32[]{:S(2)}) async-start(), calls=%async_computation.5 | async-start | bytes 589824 | tf_op jit(solution)/shard_map/psum | solution.py:15
  226.5 11.2 %collective-permute-start.11 = (bf16[1,343,768]{2,1,0:T(8,128)(2,1)S(1)}, bf16[1,343,768]{2,1,0:T(8,128)(2,1)S(1)}, u32[]{:S(2)}, u32[]{:S(2)}) collective-permute-start(bf16[1,343,768]{2,1,0:T(8,128)(2,1)S(1)} %copy.75), channel_id=1, source_target_pairs={{2,0},{3,1},{4,2},{5,3},{6,4},{7,5},{8,6},{9,7},{10,8},{11,9},{12,... | collective-permute-start | bytes 1580552 | tf_op jit(solution)/shard_map/ppermute | solution.py:22
  226.7 20.8 %copy-start.11 = (f32[4]{0:T(128)S(1)}, f32[4]{0:T(128)}, u32[]{:S(2)}) copy-start(f32[4]{0:T(128)} %get-tuple-element.149) | copy-start | bytes 52
  226.7 20.8 %copy-start.18 = (pred[2,4]{1,0:T(4,128)(4,1)S(1)}, pred[2,4]{1,0:T(4,128)(4,1)}, u32[]{:S(2)}) copy-start(pred[2,4]{1,0:T(4,128)(4,1)} %copy-done.17) | copy-start | bytes 28
  226.7 20.7 %collective-permute-start.10 = (bf16[1,343,768]{2,1,0:T(8,128)(2,1)S(1)}, bf16[1,343,768]{2,1,0:T(8,128)(2,1)S(1)}, u32[]{:S(2)}, u32[]{:S(2)}) collective-permute-start(bf16[1,343,768]{2,1,0:T(8,128)(2,1)S(1)} %copy.74), channel_id=1, source_target_pairs={{1,0},{2,1},{3,2},{4,3},{5,4},{6,5},{7,6},{8,7},{9,8},{10,9},{11,1... | collective-permute-start | bytes 1580552 | tf_op jit(solution)/shard_map/ppermute | solution.py:22
  258.1 28.9 %collective-permute-start.12 = (bf16[14,3,7,768]{3,2,1,0:T(8,128)(2,1)S(1)}, bf16[14,3,7,768]{3,2,1,0:T(8,128)(2,1)S(1)}, u32[]{:S(2)}, u32[]{:S(2)}) collective-permute-start(bf16[14,3,7,768]{3,2,1,0:T(8,128)(2,1)S(1)} %pad_maximum_fusion.11), channel_id=1, source_target_pairs={{48,0},{0,16},{16,32},{32,48},{49,1},{1,17},{17,33},{33,49},{50,2}... | collective-permute-start | bytes 1354760 | tf_op jit(solution)/shard_map/ppermute | solution.py:22
  287.9 130.8 %collective-permute-start.13 = (bf16[3,14,7,768]{3,2,1,0:T(8,128)(2,1)}, bf16[3,14,7,768]{3,2,1,0:T(8,128)(2,1)S(1)}, u32[]{:S(2)}, u32[]{:S(2)}) collective-permute-start(bf16[3,14,7,768]{3,2,1,0:T(8,128)(2,1)} %pad_maximum_fusion.10), channel_id=1, source_target_pairs={{192,0},{0,64},{64,128},{128,192},{193,1},{1,65},{65,129},{129,193... | collective-permute-start | bytes 1354760 | tf_op jit(solution)/shard_map/ppermute | solution.py:22
  371.9 102.7 %all-reduce.5.cloned.1.call-start = ((), (), s32[]{:S(2)}) async-start(), calls=%async_computation.4 | async-start | bytes 589824 | tf_op jit(solution)/shard_map/psum | solution.py:15
  (24 other events, 86.7 us)
Sparse Core Ops, SparseCore 0:
  220.9 78.6 reduce-scatter.4
  302.2 69.6 reduce-scatter.2
  374.3 44.4 all-reduce.6
  421.3 53.2 all-reduce.4
